TPU v7x, 32 devices: a whole 2x2x4 slice. The times are simulated.
32 devices in a mesh: tok: 16 (over z, x, core), head: 2 (over y).
Axes of the slice: x: 2, y: 2, z: 4, core: 2. Of those that a mesh axis runs over, the one named last changes fastest.
Arguments:
- qkv: bfloat16 [2048, 3, 7168], P(('tok', 'head')), may hold values from -80 to 80
- prefix_cache: bfloat16 [16, 256, 2, 7168], P('tok', None, None, 'head'), may hold values from -80 to 80
- suffix_lengths: int32 [16, 8], P('tok'), may hold values from 1 to 24, 128 in all within a row
- request_groups: int32 [16, 8], P('tok'), may hold values from 0 to 15, all different within a row
- prefix_owner: int32 [16], replicated, may hold values from 0 to 15, each once
Outputs:
- attended: bfloat16 [2048, 7168], P(('tok', 'head'))
- suffix_cache: bfloat16 [2048, 2, 7168], P('tok', None, 'head')
Inputs may be any that keep to these rules, and one draw needn't show every extreme that they name: `suffix_lengths`: each row sums to 128; in each row the longest request has exactly 24 tokens. `request_groups`: the 8 requests of one row belong to 8 different groups; every group is read by some request. `prefix_owner`: every slot holds exactly one group.
All inputs are finite; a program needn't handle non-finite values.
Results may differ from a plain program's by a relative error of at most 0.003.
Values may be sent and summed in bfloat16 or wider, within the bound.
A program may use at most 64 MiB of HBM per device.

v0:
```python
import math
import jax
import jax.numpy as jnp
from jax import lax
from jax.sharding import PartitionSpec as P

HD = 224


def prefix_partials(received, cache_keys, cache_values, scale):
    sources, items, width = received.shape
    heads = cache_keys.shape[1]
    query = received.reshape(sources * items, heads, width // heads)
    scores = (
        jnp.einsum("rhd,phd->hrp", query, cache_keys, preferred_element_type=jnp.float32) * scale
    )
    peak = jnp.max(scores, axis=2)
    raised = jnp.exp(scores - peak[:, :, None])
    total = jnp.sum(raised, axis=2)
    mixed = jnp.einsum(
        "hrp,phd->rhd",
        raised.astype(jnp.bfloat16),
        cache_values,
        preferred_element_type=jnp.float32,
    )
    mixed = mixed / jnp.transpose(total)[:, :, None]
    mixed = mixed.reshape(sources, items, width)
    peak = jnp.transpose(peak).reshape(sources, items, heads)
    total = jnp.transpose(total).reshape(sources, items, heads)
    return (mixed, peak, total)


def send_back(mixed, peak, total):
    return (
        lax.all_to_all(mixed, "tok", split_axis=0, concat_axis=0, tiled=True),
        lax.all_to_all(peak, "tok", split_axis=0, concat_axis=0, tiled=True),
        lax.all_to_all(total, "tok", split_axis=0, concat_axis=0, tiled=True),
    )


def per_device(qkv, prefix_cache, suffix_lengths, request_groups, prefix_owner):
    regrouped = lax.all_to_all(qkv, "head", split_axis=2, concat_axis=0, tiled=True)
    tok_rows = regrouped.shape[0]
    width = regrouped.shape[2]
    head_dim = HD
    heads = width // head_dim
    scale = 1.0 / math.sqrt(head_dim)
    query = regrouped[:, 0].reshape(tok_rows, heads, head_dim)
    keyrows = regrouped[:, 1].reshape(tok_rows, heads, head_dim)
    values = regrouped[:, 2].reshape(tok_rows, heads, head_dim)
    lengths = suffix_lengths[0]
    groups = request_groups[0]
    requests = lengths.shape[0]
    ends = jnp.cumsum(lengths)
    starts = ends - lengths
    position = jnp.arange(tok_rows, dtype=jnp.int32)
    request = jnp.sum((position[:, None] >= ends[None, :]).astype(jnp.int32), axis=1)
    scores = jnp.einsum("thd,shd->hts", query, keyrows, preferred_element_type=jnp.float32) * scale
    allowed = (request[:, None] == request[None, :]) & (position[None, :] <= position[:, None])
    scores = jnp.where(allowed[None], scores, -jnp.inf)
    peak_s = jnp.max(scores, axis=2)
    raised = jnp.exp(scores - peak_s[:, :, None])
    total_s = jnp.sum(raised, axis=2)
    mixed_s = jnp.einsum(
        "hts,shd->thd", raised.astype(jnp.bfloat16), values, preferred_element_type=jnp.float32
    )
    request_onehot = (request[:, None] == jnp.arange(requests, dtype=jnp.int32)[None, :]).astype(
        jnp.int32
    )
    token_group = jnp.sum(request_onehot * groups[None, :], axis=1)
    token_start = jnp.sum(request_onehot * starts[None, :], axis=1)
    offset = position - token_start
    owners = prefix_owner.shape[0]
    group_onehot = (token_group[:, None] == jnp.arange(owners, dtype=jnp.int32)[None, :]).astype(
        jnp.int32
    )
    slot = jnp.sum(group_onehot * prefix_owner[None, :], axis=1)
    capacity = 3 * tok_rows // lax.axis_size("tok")
    outgoing = (
        jnp.zeros((owners, capacity, width), jnp.bfloat16).at[slot, offset].set(regrouped[:, 0])
    )
    prefix_len = prefix_cache.shape[1]
    cache_keys = prefix_cache[0, :, 0].reshape(prefix_len, heads, head_dim)
    cache_values = prefix_cache[0, :, 1].reshape(prefix_len, heads, head_dim)
    received = lax.all_to_all(outgoing, "tok", split_axis=0, concat_axis=0, tiled=True)
    mixed, peak, total = prefix_partials(received, cache_keys, cache_values, scale)
    mixed_back, peak_back, total_back = send_back(mixed, peak, total)
    o_tok = mixed_back[slot, offset].reshape(tok_rows, heads, head_dim)
    m_tok = peak_back[slot, offset]
    l_tok = total_back[slot, offset]
    m_s = jnp.transpose(peak_s)
    l_s = jnp.transpose(total_s)
    top = jnp.maximum(m_tok, m_s)
    first = l_tok * jnp.exp(m_tok - top)
    second = jnp.exp(m_s - top)
    merged = (first[:, :, None] * o_tok + second[:, :, None] * mixed_s) / (first + second * l_s)[
        :, :, None
    ]
    merged = merged.reshape(tok_rows, width).astype(jnp.bfloat16)
    attended = lax.all_to_all(merged, "head", split_axis=0, concat_axis=1, tiled=True)
    suffix_cache = regrouped[:, 1:3]
    return (attended, suffix_cache)


def solution(mesh):
    in_specs = (
        P(("tok", "head"), None, None),
        P("tok", None, None, "head"),
        P("tok", None),
        P("tok", None),
        P(),
    )
    out_specs = (P(("tok", "head"), None), P("tok", None, "head"))
    return jax.shard_map(
        per_device, mesh=mesh, in_specs=in_specs, out_specs=out_specs, check_vma=False
    )
```

profile of v0, /device:TPU:10, one launch (start us, length us, event | category | flops | bytes accessed | tf_op | source)
XLA Modules:
  0.0 395.5 jit_solution(12547379650394092253)
XLA Ops:
  0.6 10.0 %copy.133 = bf16[64,3,7168]{0,1,2:T(4,128)(2,1)} copy(bf16[64,3,7168]{2,0,1:T(8,128)(2,1)} %param.5) | data formatting | bytes 5505024 | tf_op args[0]
  10.7 8.1 %reshape.146 = bf16[2,2,344064]{2,1,0:T(2,128)(2,1)} reshape(bf16[7168,3,64]{2,1,0:T(4,128)(2,1)} %bitcast.92) | data formatting | bytes 5505024
  18.7 4.0 %all-to-all-start = ((bf16[2,2,344064]{2,1,0:T(2,128)(2,1)}), bf16[2,2,344064]{2,1,0:T(2,128)(2,1)S(1)}, u32[]{:S(2)}, u32[]{:S(2)}) async-start(bf16[2,2,344064]{2,1,0:T(2,128)(2,1)} %reshape.146), calls=%async_computation | async-start | bytes 5505024 | tf_op jit(solution)/shard_map/all_to_all | solution.py:42
  23.3 31.6 %all-to-all-done = bf16[2,2,344064]{2,1,0:T(2,128)(2,1)S(1)} async-done(((bf16[2,2,344064]{2,1,0:T(2,128)(2,1)}), bf16[2,2,344064]{2,1,0:T(2,128)(2,1)S(1)}, u32[]{:S(2)}, u32[]{:S(2)}) %all-to-all-start) | async-done | bytes 2752544 | tf_op jit(solution)/shard_map/all_to_all | solution.py:42
  54.9 6.1 %reshape.147 = bf16[7168,3,64]{2,1,0:T(4,128)(2,1)} reshape(bf16[2,2,344064]{2,1,0:T(2,128)(2,1)S(1)} %all-to-all-done) | data formatting | bytes 5505024
  61.0 8.9 %copy.134 = bf16[64,3,2,3584]{3,0,2,1:T(8,128)(2,1)S(1)} copy(bf16[64,3,2,3584]{0,1,3,2:T(4,128)(2,1)} %bitcast.91) | data formatting | bytes 5505024 | tf_op jit(solution)/shard_map/all_to_all | solution.py:42
  73.5 33.3 %scatter_fusion = bf16[16,24,3584]{2,1,0:T(8,128)(2,1)} fusion(bf16[16,24,3584]{2,1,0:T(8,128)(2,1)} %broadcast_in_dim.10, s32[128]{0:T(128)S(1)} %get-tuple-element.26, bf16[128,3584]{1,0:T(8,128)(2,1)} %get-tuple-element.22), kind=kCustom, calls=%fused_computation.3 | custom fusion | bytes 2753536 | tf_op jit(solution)/shard_map/scatter | solution.py:80
  106.9 6.4 %all-to-all-start.1 = ((bf16[16,24,3584]{2,1,0:T(8,128)(2,1)}), bf16[16,24,3584]{2,1,0:T(8,128)(2,1)}, u32[]{:S(2)}, u32[]{:S(2)}) async-start(bf16[16,24,3584]{2,1,0:T(8,128)(2,1)} %scatter_fusion), calls=%async_computation.1 | async-start | bytes 5505024 | tf_op jit(solution)/shard_map/all_to_all | solution.py:85
  113.3 8.7 %fusion.30 = (bf16[1,256,1,3584]{3,2,1,0:T(2,128)(2,1)}, bf16[1,256,1,3584]{3,2,1,0:T(2,128)(2,1)}) fusion(bf16[1,256,2,3584]{3,2,1,0:T(2,128)(2,1)} %param.6), kind=kLoop, calls=%fused_computation.53 | loop fusion | bytes 7340032 | tf_op jit(solution)/shard_map/slice | solution.py:84
  122.0 8.5 %copy.135 = bf16[1,256,1,3584]{1,3,2,0:T(8,128)(2,1)} copy(bf16[1,256,1,3584]{3,2,1,0:T(2,128)(2,1)} %get-tuple-element.20) | data formatting | bytes 3670016 | tf_op jit(solution)/shard_map/slice | solution.py:83
  130.5 44.1 %all-to-all-done.1 = bf16[16,24,3584]{2,1,0:T(8,128)(2,1)} async-done(((bf16[16,24,3584]{2,1,0:T(8,128)(2,1)}), bf16[16,24,3584]{2,1,0:T(8,128)(2,1)}, u32[]{:S(2)}, u32[]{:S(2)}) %all-to-all-start.1) | async-done | bytes 2752544 | tf_op jit(solution)/shard_map/all_to_all | solution.py:85
  174.6 7.2 %reshape.117 = bf16[384,16,224]{2,1,0:T(8,128)(2,1)} reshape(bf16[16,24,3584]{2,1,0:T(8,128)(2,1)} %all-to-all-done.1) | data formatting | bytes 5505024 | tf_op jit(solution)/shard_map/reshape | solution.py:13
  181.8 5.2 %multiply_reduce_fusion = (f32[16,384]{1,0:T(8,128)S(1)}, f32[16,384,256]{1,2,0:T(8,128)S(1)}) fusion(bf16[256,16,224]{0,2,1:T(8,128)(2,1)} %bitcast.95, bf16[384,16,224]{2,1,0:T(8,128)(2,1)} %reshape.117), kind=kOutput, calls=%fused_computation.5 | convolution fusion | flops 707782656 | bytes 10903552 | tf_op jit(solution)/shard_map/rhd,phd->hrp/dot_general | solution.py:15
  190.6 5.1 %all-to-all-start.2 = ((f32[16,1,384]{2,1,0:T(1,128)}), f32[16,1,384]{2,1,0:T(1,128)S(1)}, u32[]{:S(2)}, u32[]{:S(2)}) async-start(f32[16,1,384]{2,1,0:T(1,128)} %reshape.148), calls=%async_computation.2 | async-start | bytes 49152 | tf_op jit(solution)/shard_map/all_to_all | solution.py:37
  195.7 8.5 %copy.146 = bf16[1,256,1,3584]{1,3,2,0:T(8,128)(2,1)} copy(bf16[1,256,1,3584]{3,2,1,0:T(2,128)(2,1)} %get-tuple-element.19) | data formatting | bytes 3670016 | tf_op jit(solution)/shard_map/slice | solution.py:84
  205.1 6.0 %all-to-all-start.3 = ((f32[16,1,384]{2,1,0:T(1,128)}), f32[16,1,384]{2,1,0:T(1,128)S(1)}, u32[]{:S(2)}, u32[]{:S(2)}) async-start(f32[16,1,384]{2,1,0:T(1,128)} %reshape.150), calls=%async_computation.3 | async-start | bytes 49152 | tf_op jit(solution)/shard_map/all_to_all | solution.py:36
  211.1 7.2 %bitcast_divide_fusion = f32[384,16,224]{0,2,1:T(8,128)} fusion(f32[384,16]{0,1:T(8,128)S(1)} %bitcast.108, bf16[256,16,224]{0,2,1:T(8,128)(2,1)} %bitcast.99, f32[16,384,256]{1,2,0:T(8,128)} %copy-done, f32[16,384]{1,0:T(8,128)S(1)} %get-tuple-element.27), kind=kOutput, calls=%fused_computation.6 | convolution fusion | flops 710737920 | bytes 13680640 | tf_op jit(solution)/shard_map/hrp,phd->rhd/dot_general | solution.py:20
  218.3 6.7 %copy.148 = f32[384,16,224]{2,1,0:T(8,128)} copy(f32[384,16,224]{0,2,1:T(8,128)} %bitcast_divide_fusion) | data formatting | bytes 11010048 | tf_op jit(solution)/shard_map/div | solution.py:26
  224.9 7.9 %reshape.120 = f32[16,24,3584]{2,1,0:T(8,128)} reshape(f32[384,16,224]{2,1,0:T(8,128)} %copy.148) | data formatting | bytes 11010048 | tf_op jit(solution)/shard_map/reshape | solution.py:27
  232.8 6.0 %all-to-all-start.4 = ((f32[16,24,3584]{2,1,0:T(8,128)}), f32[16,24,3584]{2,1,0:T(8,128)}, u32[]{:S(2)}, u32[]{:S(2)}) async-start(f32[16,24,3584]{2,1,0:T(8,128)} %reshape.120), calls=%async_computation.4 | async-start | bytes 11010048 | tf_op jit(solution)/shard_map/all_to_all | solution.py:35
  253.7 105.4 %all-to-all-done.4 = f32[16,24,3584]{2,1,0:T(8,128)} async-done(((f32[16,24,3584]{2,1,0:T(8,128)}), f32[16,24,3584]{2,1,0:T(8,128)}, u32[]{:S(2)}, u32[]{:S(2)}) %all-to-all-start.4) | async-done | bytes 5505056 | tf_op jit(solution)/shard_map/all_to_all | solution.py:35
  359.1 4.5 %gather_fusion.2 = f32[128,3584]{1,0:T(8,128)} fusion(f32[16,24,3584]{2,1,0:T(8,128)} %all-to-all-done.4, s32[128]{0:T(128)S(1)} %get-tuple-element.25), kind=kCustom, calls=%fused_computation.2 | custom fusion | bytes 3671040 | tf_op jit(solution)/shard_map/gather | solution.py:88
  375.9 4.4 %all-to-all-start.5 = ((bf16[2,64,3584]{2,1,0:T(8,128)(2,1)}), bf16[2,64,3584]{2,1,0:T(8,128)(2,1)}, u32[]{:S(2)}, u32[]{:S(2)}) async-start(bf16[2,64,3584]{2,1,0:T(8,128)(2,1)} %convert_element_type.22), calls=%async_computation.5 | async-start | bytes 1835008 | tf_op jit(solution)/shard_map/all_to_all | solution.py:100
  383.5 9.9 %all-to-all-done.5 = bf16[2,64,3584]{2,1,0:T(8,128)(2,1)} async-done(((bf16[2,64,3584]{2,1,0:T(8,128)(2,1)}), bf16[2,64,3584]{2,1,0:T(8,128)(2,1)}, u32[]{:S(2)}, u32[]{:S(2)}) %all-to-all-start.5) | async-done | bytes 917536 | tf_op jit(solution)/shard_map/all_to_all | solution.py:100
  (52 shorter events, 41.0 us)
Async XLA Ops:
  18.7 4.0 %copy-start.3 = (s32[1,8]{1,0:T(1,128)S(1)}, s32[1,8]{1,0:T(1,128)}, u32[]{:S(2)}) copy-start(s32[1,8]{1,0:T(1,128)} %param.7) | copy-start | bytes 100
  18.7 4.3 %copy-start.2 = (s32[1,8]{1,0:T(1,128)S(1)}, s32[1,8]{1,0:T(1,128)}, u32[]{:S(2)}) copy-start(s32[1,8]{1,0:T(1,128)} %param.8) | copy-start | bytes 100
  18.7 4.4 %copy-start.4 = (s32[16]{0:T(128)S(1)}, s32[16]{0:T(128)}, u32[]{:S(2)}) copy-start(s32[16]{0:T(128)} %param.9) | copy-start | bytes 196
  18.7 36.1 %all-to-all-start = ((bf16[2,2,344064]{2,1,0:T(2,128)(2,1)}), bf16[2,2,344064]{2,1,0:T(2,128)(2,1)S(1)}, u32[]{:S(2)}, u32[]{:S(2)}) async-start(bf16[2,2,344064]{2,1,0:T(2,128)(2,1)} %reshape.146), calls=%async_computation | async-start | bytes 5505024 | tf_op jit(solution)/shard_map/all_to_all | solution.py:42
  106.9 67.7 %all-to-all-start.1 = ((bf16[16,24,3584]{2,1,0:T(8,128)(2,1)}), bf16[16,24,3584]{2,1,0:T(8,128)(2,1)}, u32[]{:S(2)}, u32[]{:S(2)}) async-start(bf16[16,24,3584]{2,1,0:T(8,128)(2,1)} %scatter_fusion), calls=%async_computation.1 | async-start | bytes 5505024 | tf_op jit(solution)/shard_map/all_to_all | solution.py:85
  187.0 2.7 copy-start
  190.6 14.5 %all-to-all-start.2 = ((f32[16,1,384]{2,1,0:T(1,128)}), f32[16,1,384]{2,1,0:T(1,128)S(1)}, u32[]{:S(2)}, u32[]{:S(2)}) async-start(f32[16,1,384]{2,1,0:T(1,128)} %reshape.148), calls=%async_computation.2 | async-start | bytes 49152 | tf_op jit(solution)/shard_map/all_to_all | solution.py:37
  205.1 27.7 %all-to-all-start.3 = ((f32[16,1,384]{2,1,0:T(1,128)}), f32[16,1,384]{2,1,0:T(1,128)S(1)}, u32[]{:S(2)}, u32[]{:S(2)}) async-start(f32[16,1,384]{2,1,0:T(1,128)} %reshape.150), calls=%async_computation.3 | async-start | bytes 49152 | tf_op jit(solution)/shard_map/all_to_all | solution.py:36
  232.8 126.3 %all-to-all-start.4 = ((f32[16,24,3584]{2,1,0:T(8,128)}), f32[16,24,3584]{2,1,0:T(8,128)}, u32[]{:S(2)}, u32[]{:S(2)}) async-start(f32[16,24,3584]{2,1,0:T(8,128)} %reshape.120), calls=%async_computation.4 | async-start | bytes 11010048 | tf_op jit(solution)/shard_map/all_to_all | solution.py:35
  247.6 1.0 copy-start.1
  375.9 17.5 %all-to-all-start.5 = ((bf16[2,64,3584]{2,1,0:T(8,128)(2,1)}), bf16[2,64,3584]{2,1,0:T(8,128)(2,1)}, u32[]{:S(2)}, u32[]{:S(2)}) async-start(bf16[2,64,3584]{2,1,0:T(8,128)(2,1)} %convert_element_type.22), calls=%async_computation.5 | async-start | bytes 1835008 | tf_op jit(solution)/shard_map/all_to_all | solution.py:100
where the time goes:
time: 398 us; the launch traced here: 396 us
  waiting for transfers between devices  191 us (48%)
  local copies, waits for them, and re-layouts  151 us (38%)
  starting transfers between devices  31.9 us (8%)
  matrix products  17.9 us (4%)
    all_to_all x1, waiting for transfers between devices, send_back(): lax.all_to_all(mixed, 'tok', split_axis=0, concat_axis=0, tiled=True)  105 us
    all_to_all x1, waiting for transfers between devices, per_device(): lax.all_to_all(outgoing, 'tok', split_axis=0, concat_axis=0, tiled=True)  44.1 us
    scatter x1, local copies, waits for them, and re-layouts, per_device(): jnp.zeros((owners, capacity, width), jnp.bfloat16).at[slot, offset]  33.3 us
    all_to_all x1, waiting for transfers between devices, per_device(): lax.all_to_all(qkv, 'head', split_axis=2, concat_axis=0, tiled=True)  31.6 us
    unnamed x18, local copies, waits for them, and re-layouts  31.5 us
    slice x2, local copies, waits for them, and re-layouts, per_device(): cache_values = prefix_cache[0, :, 1].reshape(prefix_len, heads, head_dim)  17.2 us
    all_to_all x1, waiting for transfers between devices, per_device(): lax.all_to_all(merged, 'head', split_axis=0, concat_axis=1, tiled=True)  9.87 us
    all_to_all x1, local copies, waits for them, and re-layouts, per_device(): lax.all_to_all(qkv, 'head', split_axis=2, concat_axis=0, tiled=True)  8.86 us
  transfers between devices with their start and end apart: 6, of which 4 were waited for; matrix products, arithmetic and copies ran while one was open for 17% of the time, Pallas kernels for 0%

commit v1 on v0

--- a/solution.py
+++ b/solution.py
@@ -39,7 +39,10 @@
 
 
 def per_device(qkv, prefix_cache, suffix_lengths, request_groups, prefix_owner):
-    regrouped = lax.all_to_all(qkv, "head", split_axis=2, concat_axis=0, tiled=True)
+    regrouped = jnp.concatenate(
+        lax.all_to_all(jnp.stack(jnp.split(qkv, lax.axis_size("head"), axis=2)), "head", 0, 0),
+        axis=0,
+    )
     tok_rows = regrouped.shape[0]
     width = regrouped.shape[2]
     head_dim = HD

time: 398 us -> 371 us (0.932)
  local copies, waits for them, and re-layouts: 151 us -> 121 us
    unnamed x18 -> x15, local copies, waits for them, and re-layouts: 31.5 us -> 7.35 us
    all_to_all x1, local copies, waits for them, and re-layouts: 8.86 us -> 1.95 us  [per_device(): lax.all_to_all(jnp.stack(jnp.split(qkv, lax.axis_size('head'), axis=2)),...]
  transfers between devices with their start and end apart: 6 -> 6, of which waited for: 4 -> 4; matrix products, arithmetic and copies ran while one was open for 17% -> 18% of each run, Pallas kernels for 0% -> 0%
where the time goes in v1:
time: 371 us; the launch traced here: 369 us
  waiting for transfers between devices  191 us (51%)
  local copies, waits for them, and re-layouts  121 us (33%)
  starting transfers between devices  33.1 us (9%)
  matrix products  17.9 us (5%)
  other arithmetic  5.07 us (1%)
    all_to_all x1, waiting for transfers between devices, send_back(): lax.all_to_all(mixed, 'tok', split_axis=0, concat_axis=0, tiled=True)  105 us
    all_to_all x1, waiting for transfers between devices, per_device(): lax.all_to_all(outgoing, 'tok', split_axis=0, concat_axis=0, tiled=True)  44.1 us
    scatter x1, local copies, waits for them, and re-layouts, per_device(): jnp.zeros((owners, capacity, width), jnp.bfloat16).at[slot, offset]  33.3 us
    all_to_all x1, waiting for transfers between devices, per_device(): lax.all_to_all(jnp.stack(jnp.split(qkv, lax.axis_size('head'), axis=2)),...  31.7 us
    slice x2, local copies, waits for them, and re-layouts, per_device(): cache_values = prefix_cache[0, :, 1].reshape(prefix_len, heads, head_dim)  17.2 us
    all_to_all x1, waiting for transfers between devices, per_device(): lax.all_to_all(merged, 'head', split_axis=0, concat_axis=1, tiled=True)  9.88 us
    slice x1, local copies, waits for them, and re-layouts, per_device(): cache_keys = prefix_cache[0, :, 0].reshape(prefix_len, heads, head_dim)  8.53 us
    reshape x1, local copies, waits for them, and re-layouts, prefix_partials(): mixed = mixed.reshape(sources, items, width)  7.89 us
  transfers between devices with their start and end apart: 6, of which 4 were waited for; matrix products, arithmetic and copies ran while one was open for 18% of the time, Pallas kernels for 0%

profile of v1, /device:TPU:10, one launch (start us, length us, event | category | flops | bytes accessed | tf_op | source)
XLA Modules:
  0.0 369.5 jit_solution(2154363506061868609)
XLA Ops:
  4.4 5.2 %all-to-all-start = ((bf16[2,64,3,3584]{3,1,2,0:T(8,128)(2,1)}), bf16[2,64,3,3584]{3,1,2,0:T(8,128)(2,1)}, u32[]{:S(2)}, u32[]{:S(2)}) async-start(bf16[2,64,3,3584]{3,1,2,0:T(8,128)(2,1)} %pad_maximum_fusion), calls=%async_computation | async-start | bytes 5505024 | tf_op jit(solution)/shard_map/all_to_all | solution.py:43
  10.0 31.7 %all-to-all-done = bf16[2,64,3,3584]{3,1,2,0:T(8,128)(2,1)} async-done(((bf16[2,64,3,3584]{3,1,2,0:T(8,128)(2,1)}), bf16[2,64,3,3584]{3,1,2,0:T(8,128)(2,1)}, u32[]{:S(2)}, u32[]{:S(2)}) %all-to-all-start) | async-done | bytes 2752544 | tf_op jit(solution)/shard_map/all_to_all | solution.py:43
  47.4 33.3 %scatter_fusion = bf16[16,24,3584]{2,1,0:T(8,128)(2,1)} fusion(bf16[16,24,3584]{2,1,0:T(8,128)(2,1)} %broadcast_in_dim.10, s32[128]{0:T(128)S(1)} %get-tuple-element.28, bf16[128,3584]{1,0:T(8,128)(2,1)} %get-tuple-element.22), kind=kCustom, calls=%fused_computation.3 | custom fusion | bytes 2753536 | tf_op jit(solution)/shard_map/scatter | solution.py:83
  80.8 6.4 %all-to-all-start.1 = ((bf16[16,24,3584]{2,1,0:T(8,128)(2,1)}), bf16[16,24,3584]{2,1,0:T(8,128)(2,1)}, u32[]{:S(2)}, u32[]{:S(2)}) async-start(bf16[16,24,3584]{2,1,0:T(8,128)(2,1)} %scatter_fusion), calls=%async_computation.1 | async-start | bytes 5505024 | tf_op jit(solution)/shard_map/all_to_all | solution.py:88
  87.2 8.7 %fusion.30 = (bf16[1,256,1,3584]{3,2,1,0:T(2,128)(2,1)}, bf16[1,256,1,3584]{3,2,1,0:T(2,128)(2,1)}) fusion(bf16[1,256,2,3584]{3,2,1,0:T(2,128)(2,1)} %param.6), kind=kLoop, calls=%fused_computation.56 | loop fusion | bytes 7340032 | tf_op jit(solution)/shard_map/slice | solution.py:87
  95.9 8.5 %copy.131 = bf16[1,256,1,3584]{1,3,2,0:T(8,128)(2,1)} copy(bf16[1,256,1,3584]{3,2,1,0:T(2,128)(2,1)} %get-tuple-element.20) | data formatting | bytes 3670016 | tf_op jit(solution)/shard_map/slice | solution.py:86
  104.4 44.1 %all-to-all-done.1 = bf16[16,24,3584]{2,1,0:T(8,128)(2,1)} async-done(((bf16[16,24,3584]{2,1,0:T(8,128)(2,1)}), bf16[16,24,3584]{2,1,0:T(8,128)(2,1)}, u32[]{:S(2)}, u32[]{:S(2)}) %all-to-all-start.1) | async-done | bytes 2752544 | tf_op jit(solution)/shard_map/all_to_all | solution.py:88
  148.5 7.2 %reshape.121 = bf16[384,16,224]{2,1,0:T(8,128)(2,1)} reshape(bf16[16,24,3584]{2,1,0:T(8,128)(2,1)} %all-to-all-done.1) | data formatting | bytes 5505024 | tf_op jit(solution)/shard_map/reshape | solution.py:13
  155.7 5.2 %multiply_reduce_fusion = (f32[16,384]{1,0:T(8,128)S(1)}, f32[16,384,256]{1,2,0:T(8,128)S(1)}) fusion(bf16[256,16,224]{0,2,1:T(8,128)(2,1)} %bitcast.92, bf16[384,16,224]{2,1,0:T(8,128)(2,1)} %reshape.121), kind=kOutput, calls=%fused_computation.5 | convolution fusion | flops 707782656 | bytes 10903552 | tf_op jit(solution)/shard_map/rhd,phd->hrp/dot_general | solution.py:15
  164.5 5.1 %all-to-all-start.2 = ((f32[16,1,384]{2,1,0:T(1,128)}), f32[16,1,384]{2,1,0:T(1,128)S(1)}, u32[]{:S(2)}, u32[]{:S(2)}) async-start(f32[16,1,384]{2,1,0:T(1,128)} %reshape.150), calls=%async_computation.2 | async-start | bytes 49152 | tf_op jit(solution)/shard_map/all_to_all | solution.py:37
  169.6 8.5 %copy.142 = bf16[1,256,1,3584]{1,3,2,0:T(8,128)(2,1)} copy(bf16[1,256,1,3584]{3,2,1,0:T(2,128)(2,1)} %get-tuple-element.19) | data formatting | bytes 3670016 | tf_op jit(solution)/shard_map/slice | solution.py:87
  179.0 6.0 %all-to-all-start.3 = ((f32[16,1,384]{2,1,0:T(1,128)}), f32[16,1,384]{2,1,0:T(1,128)S(1)}, u32[]{:S(2)}, u32[]{:S(2)}) async-start(f32[16,1,384]{2,1,0:T(1,128)} %reshape.152), calls=%async_computation.3 | async-start | bytes 49152 | tf_op jit(solution)/shard_map/all_to_all | solution.py:36
  185.0 7.2 %bitcast_divide_fusion = f32[384,16,224]{0,2,1:T(8,128)} fusion(f32[384,16]{0,1:T(8,128)S(1)} %bitcast.105, bf16[256,16,224]{0,2,1:T(8,128)(2,1)} %bitcast.96, f32[16,384,256]{1,2,0:T(8,128)} %copy-done, f32[16,384]{1,0:T(8,128)S(1)} %get-tuple-element.29), kind=kOutput, calls=%fused_computation.6 | convolution fusion | flops 710737920 | bytes 13680640 | tf_op jit(solution)/shard_map/hrp,phd->rhd/dot_general | solution.py:20
  192.2 6.7 %copy.144 = f32[384,16,224]{2,1,0:T(8,128)} copy(f32[384,16,224]{0,2,1:T(8,128)} %bitcast_divide_fusion) | data formatting | bytes 11010048 | tf_op jit(solution)/shard_map/div | solution.py:26
  198.9 7.9 %reshape.124 = f32[16,24,3584]{2,1,0:T(8,128)} reshape(f32[384,16,224]{2,1,0:T(8,128)} %copy.144) | data formatting | bytes 11010048 | tf_op jit(solution)/shard_map/reshape | solution.py:27
  206.7 6.0 %all-to-all-start.4 = ((f32[16,24,3584]{2,1,0:T(8,128)}), f32[16,24,3584]{2,1,0:T(8,128)}, u32[]{:S(2)}, u32[]{:S(2)}) async-start(f32[16,24,3584]{2,1,0:T(8,128)} %reshape.124), calls=%async_computation.4 | async-start | bytes 11010048 | tf_op jit(solution)/shard_map/all_to_all | solution.py:35
  227.7 105.4 %all-to-all-done.4 = f32[16,24,3584]{2,1,0:T(8,128)} async-done(((f32[16,24,3584]{2,1,0:T(8,128)}), f32[16,24,3584]{2,1,0:T(8,128)}, u32[]{:S(2)}, u32[]{:S(2)}) %all-to-all-start.4) | async-done | bytes 5505056 | tf_op jit(solution)/shard_map/all_to_all | solution.py:35
  333.0 4.5 %gather_fusion.2 = f32[128,3584]{1,0:T(8,128)} fusion(f32[16,24,3584]{2,1,0:T(8,128)} %all-to-all-done.4, s32[128]{0:T(128)S(1)} %get-tuple-element.27), kind=kCustom, calls=%fused_computation.2 | custom fusion | bytes 3671040 | tf_op jit(solution)/shard_map/gather | solution.py:91
  337.6 2.7 copy.145
  340.3 3.6 fusion.10
  346.5 3.3 convert_element_type.22
  349.8 4.4 %all-to-all-start.5 = ((bf16[2,64,3584]{2,1,0:T(8,128)(2,1)}), bf16[2,64,3584]{2,1,0:T(8,128)(2,1)}, u32[]{:S(2)}, u32[]{:S(2)}) async-start(bf16[2,64,3584]{2,1,0:T(8,128)(2,1)} %convert_element_type.22), calls=%async_computation.5 | async-start | bytes 1835008 | tf_op jit(solution)/shard_map/all_to_all | solution.py:103
  354.3 3.1 copy.150
  357.4 9.9 %all-to-all-done.5 = bf16[2,64,3584]{2,1,0:T(8,128)(2,1)} async-done(((bf16[2,64,3584]{2,1,0:T(8,128)(2,1)}), bf16[2,64,3584]{2,1,0:T(8,128)(2,1)}, u32[]{:S(2)}, u32[]{:S(2)}) %all-to-all-start.5) | async-done | bytes 917536 | tf_op jit(solution)/shard_map/all_to_all | solution.py:103
  (51 shorter events, 34.0 us)
Async XLA Ops:
  4.4 5.2 %copy-start.3 = (s32[1,8]{1,0:T(1,128)S(1)}, s32[1,8]{1,0:T(1,128)}, u32[]{:S(2)}) copy-start(s32[1,8]{1,0:T(1,128)} %param.7) | copy-start | bytes 100
  4.4 5.5 %copy-start.2 = (s32[1,8]{1,0:T(1,128)S(1)}, s32[1,8]{1,0:T(1,128)}, u32[]{:S(2)}) copy-start(s32[1,8]{1,0:T(1,128)} %param.8) | copy-start | bytes 100
  4.4 5.6 %copy-start.4 = (s32[16]{0:T(128)S(1)}, s32[16]{0:T(128)}, u32[]{:S(2)}) copy-start(s32[16]{0:T(128)} %param.9) | copy-start | bytes 196
  4.4 37.4 %all-to-all-start = ((bf16[2,64,3,3584]{3,1,2,0:T(8,128)(2,1)}), bf16[2,64,3,3584]{3,1,2,0:T(8,128)(2,1)}, u32[]{:S(2)}, u32[]{:S(2)}) async-start(bf16[2,64,3,3584]{3,1,2,0:T(8,128)(2,1)} %pad_maximum_fusion), calls=%async_computation | async-start | bytes 5505024 | tf_op jit(solution)/shard_map/all_to_all | solution.py:43
  80.8 67.7 %all-to-all-start.1 = ((bf16[16,24,3584]{2,1,0:T(8,128)(2,1)}), bf16[16,24,3584]{2,1,0:T(8,128)(2,1)}, u32[]{:S(2)}, u32[]{:S(2)}) async-start(bf16[16,24,3584]{2,1,0:T(8,128)(2,1)} %scatter_fusion), calls=%async_computation.1 | async-start | bytes 5505024 | tf_op jit(solution)/shard_map/all_to_all | solution.py:88
  160.9 2.7 copy-start
  164.5 14.5 %all-to-all-start.2 = ((f32[16,1,384]{2,1,0:T(1,128)}), f32[16,1,384]{2,1,0:T(1,128)S(1)}, u32[]{:S(2)}, u32[]{:S(2)}) async-start(f32[16,1,384]{2,1,0:T(1,128)} %reshape.150), calls=%async_computation.2 | async-start | bytes 49152 | tf_op jit(solution)/shard_map/all_to_all | solution.py:37
  179.0 27.7 %all-to-all-start.3 = ((f32[16,1,384]{2,1,0:T(1,128)}), f32[16,1,384]{2,1,0:T(1,128)S(1)}, u32[]{:S(2)}, u32[]{:S(2)}) async-start(f32[16,1,384]{2,1,0:T(1,128)} %reshape.152), calls=%async_computation.3 | async-start | bytes 49152 | tf_op jit(solution)/shard_map/all_to_all | solution.py:36
  206.7 126.3 %all-to-all-start.4 = ((f32[16,24,3584]{2,1,0:T(8,128)}), f32[16,24,3584]{2,1,0:T(8,128)}, u32[]{:S(2)}, u32[]{:S(2)}) async-start(f32[16,24,3584]{2,1,0:T(8,128)} %reshape.124), calls=%async_computation.4 | async-start | bytes 11010048 | tf_op jit(solution)/shard_map/all_to_all | solution.py:35
  221.5 1.0 copy-start.1
  349.8 17.5 %all-to-all-start.5 = ((bf16[2,64,3584]{2,1,0:T(8,128)(2,1)}), bf16[2,64,3584]{2,1,0:T(8,128)(2,1)}, u32[]{:S(2)}, u32[]{:S(2)}) async-start(bf16[2,64,3584]{2,1,0:T(8,128)(2,1)} %convert_element_type.22), calls=%async_computation.5 | async-start | bytes 1835008 | tf_op jit(solution)/shard_map/all_to_all | solution.py:103
